TPU v7x, 256 devices: a whole 4x4x8 slice. The times are simulated.
256 devices in a mesh: pl: 16 (over y, x), xs: 16 (over z, core).
Axes of the slice: x: 4, y: 4, z: 8, core: 2. Of those that a mesh axis runs over, the one named last changes fastest.
Arguments:
- source: float32 [512, 16, 2048], P('xs', None, 'pl'), may hold values from -6 to 6
- eastward_rate: float32 [512, 16, 2048], P('xs', None, 'pl'), may hold values from 300 to 6000
- northward_rate: float32 [512, 16, 2048], P('xs', None, 'pl'), may hold values from 300 to 6000
- vertical_rate: float32 [512, 16, 2048], P('xs', None, 'pl'), may hold values from 0.5 to 20
- amplitude: float32 [512, 16, 2048], P('xs', None, 'pl'), may hold values from 300 to 3000
Outputs:
- smoothed: float32 [512, 16, 2048], P('xs', None, 'pl')
All inputs are finite; a program needn't handle non-finite values.
Results may differ from a plain program's by a relative error of at most 0.0003.
Values sent between devices are 32-bit elements; how exact they have to be, the bound alone decides.
A program may use at most 128 MiB of HBM per device.

v0:
```python
import jax
import jax.numpy as jnp
from jax import lax
from jax.sharding import PartitionSpec as P


def cyclic(sub_band, centre, super_band, values):
    length = centre.shape[0]
    if length == 1:
        return values / centre

    def halves(operand):
        paired = operand.reshape((length // 2, 2) + operand.shape[1:])
        return (paired[:, 0], paired[:, 1])

    def following(operand, filler):
        return jnp.concatenate([operand[1:], jnp.full_like(operand[:1], filler)], axis=0)

    sub_even, sub_odd = halves(sub_band)
    centre_even, centre_odd = halves(centre)
    super_even, super_odd = halves(super_band)
    values_even, values_odd = halves(values)
    left_factor = -sub_odd / centre_even
    right_factor = -super_odd / following(centre_even, 1.0)
    reduced = cyclic(
        left_factor * sub_even,
        centre_odd + left_factor * super_even + right_factor * following(sub_even, 0.0),
        right_factor * following(super_even, 0.0),
        values_odd + left_factor * values_even + right_factor * following(values_even, 0.0),
    )
    previous = jnp.concatenate([jnp.zeros_like(reduced[:1]), reduced[:-1]], axis=0)
    even_part = (values_even - sub_even * previous - super_even * reduced) / centre_even
    return jnp.stack([even_part, reduced], axis=1).reshape((length,) + even_part.shape[1:])


def cyclic_last(sub_band, centre, super_band, values):
    length = centre.shape[-1]
    if length == 1:
        return values / centre

    def halves(operand):
        paired = operand.reshape(operand.shape[:-1] + (length // 2, 2))
        return (paired[..., 0], paired[..., 1])

    def following(operand, filler):
        return jnp.concatenate([operand[..., 1:], jnp.full_like(operand[..., :1], filler)], axis=-1)

    sub_even, sub_odd = halves(sub_band)
    centre_even, centre_odd = halves(centre)
    super_even, super_odd = halves(super_band)
    values_even, values_odd = halves(values)
    left_factor = -sub_odd / centre_even
    right_factor = -super_odd / following(centre_even, 1.0)
    reduced = cyclic_last(
        left_factor * sub_even,
        centre_odd + left_factor * super_even + right_factor * following(sub_even, 0.0),
        right_factor * following(super_even, 0.0),
        values_odd + left_factor * values_even + right_factor * following(values_even, 0.0),
    )
    previous = jnp.concatenate([jnp.zeros_like(reduced[..., :1]), reduced[..., :-1]], axis=-1)
    even_part = (values_even - sub_even * previous - super_even * reduced) / centre_even
    return jnp.stack([even_part, reduced], axis=-1).reshape(even_part.shape[:-1] + (length,))


def band_solve(values, rate_lines):
    length = values.shape[0]
    position = lax.broadcasted_iota(jnp.int32, rate_lines.shape, 0)
    sub_band = jnp.where(position > 0, -rate_lines, 0.0)
    super_band = jnp.where(position < length - 1, -rate_lines, 0.0)
    return cyclic(sub_band, 1.0 + 2.0 * rate_lines, super_band, values)


def vertical_solve(values, vertical_lines):
    return jnp.moveaxis(band_solve(jnp.moveaxis(values, 1, 0), vertical_lines), 0, 1)


def northward_solve(values, north_lines):
    length = values.shape[-1]
    position = lax.broadcasted_iota(jnp.int32, north_lines.shape, 2)
    sub_band = jnp.where(position > 0, -north_lines, 0.0)
    super_band = jnp.where(position < length - 1, -north_lines, 0.0)
    return cyclic_last(sub_band, 1.0 + 2.0 * north_lines, super_band, values)


def to_lines(values):
    return lax.all_to_all(values, "pl", split_axis=1, concat_axis=2, tiled=True)


def to_planes(values):
    return lax.all_to_all(values, "pl", split_axis=2, concat_axis=1, tiled=True)


def matrix_product(left_matrix, right_matrix):
    return (
        left_matrix[0] * right_matrix[0] + left_matrix[1] * right_matrix[2],
        left_matrix[0] * right_matrix[1] + left_matrix[1] * right_matrix[3],
        left_matrix[2] * right_matrix[0] + left_matrix[3] * right_matrix[2],
        left_matrix[2] * right_matrix[1] + left_matrix[3] * right_matrix[3],
    )


def matrix_inverse(matrix):
    determinant = matrix[0] * matrix[3] - matrix[1] * matrix[2]
    return (
        matrix[3] / determinant,
        -matrix[1] / determinant,
        -matrix[2] / determinant,
        matrix[0] / determinant,
    )


def matrix_vector(matrix, vector):
    return (
        matrix[0] * vector[0] + matrix[1] * vector[1],
        matrix[2] * vector[0] + matrix[3] * vector[1],
    )


def unpack_rows(packed):
    sub_block = (packed[0], packed[1], packed[2], packed[3])
    centre = (packed[4] + 1.0, packed[5], packed[6], packed[7] + 1.0)
    super_block = (packed[8], packed[9], packed[10], packed[11])
    right_side = (packed[12], packed[13])
    return (sub_block, centre, super_block, right_side)


def pack_rows(sub_block, centre, super_block, right_side):
    return jnp.stack(
        [
            sub_block[0],
            sub_block[1],
            sub_block[2],
            sub_block[3],
            centre[0] - 1.0,
            centre[1],
            centre[2],
            centre[3] - 1.0,
            super_block[0],
            super_block[1],
            super_block[2],
            super_block[3],
            right_side[0],
            right_side[1],
        ]
    )


def first_rows(boundary):
    blank_rows = jnp.zeros_like(boundary[0])
    return jnp.stack(
        [
            blank_rows,
            boundary[0],
            blank_rows,
            boundary[1],
            blank_rows,
            blank_rows,
            blank_rows,
            blank_rows,
            boundary[2],
            blank_rows,
            boundary[3],
            blank_rows,
            boundary[4],
            boundary[5],
        ]
    )


def eliminate(own_rows, rows_below, rows_above):
    sub_block, centre, super_block, right_side = unpack_rows(own_rows)
    sub_below, centre_below, super_below, right_below = unpack_rows(rows_below)
    sub_above, centre_above, super_above, right_above = unpack_rows(rows_above)
    left_factor = matrix_product(sub_block, matrix_inverse(centre_below))
    right_factor = matrix_product(super_block, matrix_inverse(centre_above))
    new_sub = tuple((-entry for entry in matrix_product(left_factor, sub_below)))
    new_super = tuple((-entry for entry in matrix_product(right_factor, super_above)))
    left_part = matrix_product(left_factor, super_below)
    right_part = matrix_product(right_factor, sub_above)
    new_centre = tuple((centre[slot] - left_part[slot] - right_part[slot] for slot in range(4)))
    left_vector = matrix_vector(left_factor, right_below)
    right_vector = matrix_vector(right_factor, right_above)
    new_right = (
        right_side[0] - left_vector[0] - right_vector[0],
        right_side[1] - left_vector[1] - right_vector[1],
    )
    return pack_rows(new_sub, new_centre, new_super, new_right)


def finish_rows(packed):
    sub_block, centre, super_block, right_side = unpack_rows(packed)
    return matrix_vector(matrix_inverse(centre), right_side)


def solve_gathered(gathered, own_index, devices):
    row_blocks = first_rows(jnp.moveaxis(gathered, 0, 1))
    stride = 1
    while stride < devices:
        blank_rows = jnp.zeros_like(row_blocks[:, :stride])
        rows_below = jnp.concatenate([blank_rows, row_blocks[:, :-stride]], axis=1)
        rows_above = jnp.concatenate([row_blocks[:, stride:], blank_rows], axis=1)
        row_blocks = eliminate(row_blocks, rows_below, rows_above)
        stride = stride * 2
    first_value, last_value = finish_rows(row_blocks)
    blank_value = jnp.zeros_like(first_value[:1])
    padded_first = jnp.concatenate([blank_value, first_value, blank_value], axis=0)
    padded_last = jnp.concatenate([blank_value, last_value, blank_value], axis=0)
    last_before = lax.dynamic_index_in_dim(padded_last, own_index, 0, keepdims=False)
    first_after = lax.dynamic_index_in_dim(padded_first, own_index + 2, 0, keepdims=False)
    return (last_before, first_after)


def coupled(boundary):
    devices = lax.axis_size("xs")
    gathered = lax.all_gather(boundary[None], "xs", axis=0, tiled=True)
    last_before, first_after = solve_gathered(gathered, lax.axis_index("xs"), devices)
    return (last_before, first_after)


def spike_parts(values, rate, own_index, devices):
    length = values.shape[0]
    position = lax.broadcasted_iota(jnp.int32, values.shape, 0)
    sub_band = jnp.where(position > 0, -rate, 0.0)
    super_band = jnp.where(position < length - 1, -rate, 0.0)
    centre = 1.0 + 2.0 * rate
    left_edge = jnp.where((position == 0) & (own_index > 0), -rate, 0.0)
    right_edge = jnp.where((position == length - 1) & (own_index < devices - 1), -rate, 0.0)
    stacked = jnp.stack([values, left_edge, right_edge], axis=1)
    solved = cyclic(sub_band[:, None], centre[:, None], super_band[:, None], stacked)
    particular = solved[:, 0]
    spike_left = solved[:, 1]
    spike_right = solved[:, 2]
    boundary = jnp.stack(
        [
            spike_left[0],
            spike_left[-1],
            spike_right[0],
            spike_right[-1],
            particular[0],
            particular[-1],
        ]
    )
    return (particular, spike_left, spike_right, boundary)


def eastward_solve(values, east_rate):
    particular, spike_left, spike_right, boundary = spike_parts(
        values, east_rate, lax.axis_index("xs"), lax.axis_size("xs")
    )
    last_before, first_after = coupled(boundary)
    return particular - spike_left * last_before[None] - spike_right * first_after[None]


def shards(source, eastward_rate, northward_rate, vertical_rate, amplitude):
    vertical_lines = jnp.moveaxis(vertical_rate, 1, 0)
    values = vertical_solve(source, vertical_lines)
    north_lines = lax.all_to_all(northward_rate, "pl", split_axis=1, concat_axis=2, tiled=True)
    values = to_planes(northward_solve(to_lines(values), north_lines))
    values = eastward_solve(values, eastward_rate)
    values = eastward_solve(values, eastward_rate)
    values = to_planes(northward_solve(to_lines(values), north_lines))
    values = vertical_solve(values, vertical_lines)
    return amplitude * values


def solution(mesh):
    placed = (
        P("xs", None, "pl"),
        P("xs", None, "pl"),
        P("xs", None, "pl"),
        P("xs", None, "pl"),
        P("xs", None, "pl"),
    )
    return jax.shard_map(
        shards, mesh=mesh, in_specs=placed, out_specs=P("xs", None, "pl"), check_vma=False
    )
```

profile of v0, /device:TPU:32, one launch (start us, length us, event | category | flops | bytes accessed | tf_op | source)
XLA Modules:
  0.0 218.9 jit_solution(4738351005885732317)
XLA Ops:
  3.7 7.0 %all-to-all-start = ((f32[32,16,128]{2,0,1:T(8,128)}), f32[32,16,128]{2,0,1:T(8,128)S(1)}, u32[]{:S(2)}, u32[]{:S(2)}) async-start(f32[32,16,128]{2,0,1:T(8,128)} %bitcast.68), calls=%async_computation | async-start | bytes 524288 | tf_op jit(solution)/shard_map/all_to_all | solution.py:86
  27.6 7.4 %all-to-all-start.1 = ((f32[32,16,128]{2,0,1:T(8,128)}), f32[32,16,128]{2,0,1:T(8,128)S(1)}, u32[]{:S(2)}, u32[]{:S(2)}) async-start(f32[32,16,128]{2,0,1:T(8,128)} %copy.1550), calls=%async_computation.1 | async-start | bytes 524288 | tf_op jit(solution)/shard_map/all_to_all | solution.py:257
  35.3 1.6 fusion.580
  37.8 5.9 %all-to-all-done.1 = f32[32,16,128]{2,0,1:T(8,128)S(1)} async-done(((f32[32,16,128]{2,0,1:T(8,128)}), f32[32,16,128]{2,0,1:T(8,128)S(1)}, u32[]{:S(2)}, u32[]{:S(2)}) %all-to-all-start.1) | async-done | bytes 262176 | tf_op jit(solution)/shard_map/all_to_all | solution.py:257
  44.1 1.6 fusion.579
  47.2 2.6 %copy_select_fusion = (f32[32,1,1024,2]{0,2,3,1:T(8,128)S(1)}, f32[32,1,1024,2]{0,2,3,1:T(8,128)S(1)}) fusion(f32[32,1,1024,2]{0,3,2,1:T(2,128)} %bitcast.4710, pred[1024,2]{0,1:T(4,128)(4,1)S(1)} %get-tuple-element.502, pred[1024,2]{0,1:T(4,128)(4,1)S(1)} %get-tuple-element.503), kind=kLoop, calls=%fused_computation.210 | loop fusion | flops 131072 | bytes 790528 | tf_op jit(solution)/shard_map/jit(_where)/select_n | solution.py:81
  61.8 1.9 copy.1628
  64.2 11.6 %reduce = f32[2048,32]{1,0:T(8,128)} reduce(f32[2048,1,32]{2,1,0:T(1,128)} %bitcast.4714, f32[]{:T(128)} %broadcast.2033), dimensions={1}, to_apply=%bitcast.4048.reduce_sub_computation | reduce | bytes 524292
  75.8 2.4 %reshape.3598 = f32[16,1,4096]{2,1,0:T(1,128)} reshape(f32[2048,32]{1,0:T(8,128)} %reduce) | data formatting | bytes 524288
  78.2 4.2 %all-to-all-start.2 = ((f32[16,1,4096]{2,1,0:T(1,128)}), f32[16,1,4096]{2,1,0:T(1,128)}, u32[]{:S(2)}, u32[]{:S(2)}) async-start(f32[16,1,4096]{2,1,0:T(1,128)} %reshape.3598), calls=%async_computation.2 | async-start | bytes 524288 | tf_op jit(solution)/shard_map/all_to_all | solution.py:90
  85.1 1.8 bitcast_divide_fusion.61
  86.9 4.2 %all-to-all-done.2 = f32[16,1,4096]{2,1,0:T(1,128)} async-done(((f32[16,1,4096]{2,1,0:T(1,128)}), f32[16,1,4096]{2,1,0:T(1,128)}, u32[]{:S(2)}, u32[]{:S(2)}) %all-to-all-start.2) | async-done | bytes 262176 | tf_op jit(solution)/shard_map/all_to_all | solution.py:90
  91.1 2.9 %reduce.1 = f32[16,4096]{1,0:T(8,128)} reduce(f32[16,1,4096]{2,1,0:T(1,128)} %all-to-all-done.2, f32[]{:T(128)} %broadcast.2033), dimensions={1}, to_apply=%all_to_all.14.reduce_sub_computation | reduce | bytes 524292 | tf_op jit(solution)/shard_map/all_to_all | solution.py:90
  93.9 3.7 %reshape.3599 = f32[2048,1,32]{2,1,0:T(1,128)} reshape(f32[16,4096]{1,0:T(8,128)} %reduce.1) | data formatting | bytes 524288
  97.7 3.4 %copy.1630 = f32[32,1,2048]{2,1,0:T(1,128)} copy(f32[32,1,2048]{0,1,2:T(1,128)} %bitcast.4711) | data formatting | bytes 524288 | tf_op jit(solution)/shard_map/all_to_all | solution.py:90
  104.9 20.5 %all-gather = f32[96,16,128]{2,1,0:T(8,128)S(1)} all-gather(f32[6,16,128]{2,1,0:T(8,128)S(1)} %constant_dynamic-update-slice_fusion), channel_id=2, replica_groups=mesh['pl'=16,'xs'=16] {'xs'}, dimensions={0}, use_global_device_ids=true | all-gather | bytes 835584 | tf_op jit(solution)/shard_map/all_gather | solution.py:215
  130.9 5.1 %fusion.406 = (f32[16,16,128]{2,1,0:T(8,128)S(1)}, f32[16,16,128]{2,1,0:T(8,128)S(1)}, f32[16,16,128]{2,1,0:T(8,128)S(1)}, f32[16,16,128]{2,1,0:T(8,128)S(1)}, f...) fusion(f32[16,16,128]{2,1,0:T(8,128)S(1)} %get-tuple-element.322, ...), kind=kLoop, calls=%fused_computation.1275 | loop fusion | flops 23101440 | bytes 16613376 | tf_op jit(solution)/shard_map/add | solution.py:115
  138.8 18.6 %all-gather.1 = f32[96,16,128]{2,1,0:T(8,128)S(1)} all-gather(f32[6,16,128]{2,1,0:T(8,128)S(1)} %constant_dynamic-update-slice_fusion.56), channel_id=3, replica_groups=mesh['pl'=16,'xs'=16] {'xs'}, dimensions={0}, use_global_device_ids=true | all-gather | bytes 835584 | tf_op jit(solution)/shard_map/all_gather | solution.py:215
  162.9 5.0 %fusion.403 = (f32[16,16,128]{2,1,0:T(8,128)S(1)}, f32[16,16,128]{2,1,0:T(8,128)S(1)}, f32[16,16,128]{2,1,0:T(8,128)S(1)}, f32[16,16,128]{2,1,0:T(8,128)S(1)}, f...) fusion(f32[16,16,128]{2,1,0:T(8,128)S(1)} %get-tuple-element.316, ...), kind=kLoop, calls=%fused_computation.1183 | loop fusion | flops 23101440 | bytes 16613376 | tf_op jit(solution)/shard_map/add | solution.py:115
  168.2 12.3 %all_to_all.23 = f32[32,16,128]{2,0,1:T(8,128)S(1)} all-to-all(f32[32,16,128]{2,0,1:T(8,128)S(1)} %copy.1714), channel_id=1, replica_groups=mesh['pl'=16,'xs'=16] {'pl'}, dimensions={1} | all-to-all | bytes 524288 | tf_op jit(solution)/shard_map/all_to_all | solution.py:86
  181.8 2.5 %fusion.578 = (f32[32,1,1024,1]{0,3,2,1:T(1,128)S(1)}, f32[32,1,1024,1]{0,3,2,1:T(1,128)S(1)}) fusion(f32[32,1,1024,2]{0,3,2,1:T(2,128)} %bitcast.4715), kind=kLoop, calls=%fused_computation.1763 | loop fusion | bytes 524288 | tf_op jit(solution)/shard_map/slice | solution.py:43
  190.6 9.3 %reduce.2 = f32[2048,32]{1,0:T(8,128)S(1)} reduce(f32[2048,1,32]{2,1,0:T(1,128)S(1)} %bitcast.4716, f32[]{:T(128)} %broadcast.2033), dimensions={1}, to_apply=%bitcast.4050.reduce_sub_computation | reduce | bytes 524292
  200.4 11.8 %all_to_all.24 = f32[16,1,4096]{2,1,0:T(1,128)S(1)} all-to-all(f32[16,1,4096]{2,1,0:T(1,128)S(1)} %reshape.3600), channel_id=1, replica_groups=mesh['pl'=16,'xs'=16] {'pl'}, dimensions={0} | all-to-all | bytes 524288 | tf_op jit(solution)/shard_map/all_to_all | solution.py:90
  213.4 1.8 reshape.3601
  (894 shorter events, 63.7 us)
Async XLA Ops:
  2.3 8.4 %copy-start.113 = (f32[32,16,128]{2,1,0:T(8,128)S(1)}, f32[32,16,128]{2,1,0:T(8,128)}, u32[]{:S(2)}) copy-start(f32[32,16,128]{2,1,0:T(8,128)} %param.6) | copy-start | bytes 786436
  3.7 23.9 %all-to-all-start = ((f32[32,16,128]{2,0,1:T(8,128)}), f32[32,16,128]{2,0,1:T(8,128)S(1)}, u32[]{:S(2)}, u32[]{:S(2)}) async-start(f32[32,16,128]{2,0,1:T(8,128)} %bitcast.68), calls=%async_computation | async-start | bytes 524288 | tf_op jit(solution)/shard_map/all_to_all | solution.py:86
  13.6 12.6 %copy-start.112 = (f32[32,16,128]{2,1,0:T(8,128)S(1)}, f32[32,16,128]{2,1,0:T(8,128)}, u32[]{:S(2)}) copy-start(f32[32,16,128]{2,1,0:T(8,128)} %param.7) | copy-start | bytes 786436
  27.6 16.1 %all-to-all-start.1 = ((f32[32,16,128]{2,0,1:T(8,128)}), f32[32,16,128]{2,0,1:T(8,128)S(1)}, u32[]{:S(2)}, u32[]{:S(2)}) async-start(f32[32,16,128]{2,0,1:T(8,128)} %copy.1550), calls=%async_computation.1 | async-start | bytes 524288 | tf_op jit(solution)/shard_map/all_to_all | solution.py:257
  52.8 8.1 %copy-start.2 = (f32[32,1,512,1]{0,3,2,1:T(1,128)}, f32[32,1,512,1]{0,3,2,1:T(1,128)S(1)}, u32[]{:S(2)}) copy-start(f32[32,1,512,1]{0,3,2,1:T(1,128)S(1)} %get-tuple-element.347) | copy-start | bytes 196612
  53.3 7.6 %copy-start.4 = (f32[32,1,512,1]{0,3,2,1:T(1,128)}, f32[32,1,512,1]{0,3,2,1:T(1,128)S(1)}, u32[]{:S(2)}) copy-start(f32[32,1,512,1]{0,3,2,1:T(1,128)S(1)} %get-tuple-element.343) | copy-start | bytes 196612
  54.6 5.9 %copy-start.16 = (f32[32,1,256,1]{0,3,2,1:T(1,128)}, f32[32,1,256,1]{0,3,2,1:T(1,128)S(1)}, u32[]{:S(2)}) copy-start(f32[32,1,256,1]{0,3,2,1:T(1,128)S(1)} %get-tuple-element.372) | copy-start | bytes 98308
  54.8 5.7 %copy-start.18 = (f32[32,1,256,1]{0,3,2,1:T(1,128)}, f32[32,1,256,1]{0,3,2,1:T(1,128)S(1)}, u32[]{:S(2)}) copy-start(f32[32,1,256,1]{0,3,2,1:T(1,128)S(1)} %get-tuple-element.368) | copy-start | bytes 98308
  55.3 5.0 %copy-start.14 = (f32[32,1,128,1]{0,3,2,1:T(1,128)}, f32[32,1,128,1]{0,3,2,1:T(1,128)S(1)}, u32[]{:S(2)}) copy-start(f32[32,1,128,1]{0,3,2,1:T(1,128)S(1)} %get-tuple-element.399) | copy-start | bytes 49156
  55.7 4.6 %copy-start.41 = (f32[32,1,128,1]{0,3,2,1:T(1,128)}, f32[32,1,128,1]{0,3,2,1:T(1,128)S(1)}, u32[]{:S(2)}) copy-start(f32[32,1,128,1]{0,3,2,1:T(1,128)S(1)} %get-tuple-element.400) | copy-start | bytes 49156
  55.8 4.5 %copy-start.43 = (f32[32,1,128,1]{0,3,2,1:T(1,128)}, f32[32,1,128,1]{0,3,2,1:T(1,128)S(1)}, u32[]{:S(2)}) copy-start(f32[32,1,128,1]{0,3,2,1:T(1,128)S(1)} %get-tuple-element.396) | copy-start | bytes 49156
  56.1 4.0 %copy-start.35 = (f32[32,1,64,1]{0,3,2,1:T(1,128)}, f32[32,1,64,1]{0,3,2,1:T(1,128)S(1)}, u32[]{:S(2)}) copy-start(f32[32,1,64,1]{0,3,2,1:T(1,128)S(1)} %get-tuple-element.417) | copy-start | bytes 24580
  56.6 3.6 %copy-start.67 = (f32[32,1,64,1]{0,3,2,1:T(1,128)}, f32[32,1,64,1]{0,3,2,1:T(1,128)S(1)}, u32[]{:S(2)}) copy-start(f32[32,1,64,1]{0,3,2,1:T(1,128)S(1)} %get-tuple-element.418) | copy-start | bytes 24580
  56.6 3.6 %copy-start.71 = (f32[32,1,64,1]{0,3,2,1:T(1,128)}, f32[32,1,64,1]{0,3,2,1:T(1,128)S(1)}, u32[]{:S(2)}) copy-start(f32[32,1,64,1]{0,3,2,1:T(1,128)S(1)} %get-tuple-element.419) | copy-start | bytes 24580
  56.7 3.7 %copy-start.69 = (f32[32,1,64,1]{0,3,2,1:T(1,128)}, f32[32,1,64,1]{0,3,2,1:T(1,128)S(1)}, u32[]{:S(2)}) copy-start(f32[32,1,64,1]{0,3,2,1:T(1,128)S(1)} %get-tuple-element.414) | copy-start | bytes 24580
  56.7 3.7 %copy-start.100 = (f32[32,1,64]{0,2,1:T(8,128)}, f32[32,1,64]{0,2,1:T(8,128)S(1)}, u32[]{:S(2)}) copy-start(f32[32,1,64]{0,2,1:T(8,128)S(1)} %get-tuple-element.236) | copy-start | bytes 24580
  56.9 3.2 %copy-start.88 = (f32[32,1,32,1]{0,3,2,1:T(1,128)}, f32[32,1,32,1]{0,3,2,1:T(1,128)S(1)}, u32[]{:S(2)}) copy-start(f32[32,1,32,1]{0,3,2,1:T(1,128)S(1)} %get-tuple-element.434) | copy-start | bytes 12292
  64.2 18.8 %copy-start.60 = (f32[16,1,1,16,128]{4,1,0,3,2:T(1,128)S(1)}, f32[16,1,1,16,128]{4,1,0,3,2:T(1,128)}, u32[]{:S(2)}) copy-start(f32[16,1,1,16,128]{4,1,0,3,2:T(1,128)} %copy-done.59) | copy-start | bytes 393220
  64.2 19.5 %copy-start.64 = (f32[32,16,128]{2,0,1:T(8,128)S(1)}, f32[32,16,128]{2,0,1:T(8,128)}, u32[]{:S(2)}) copy-start(f32[32,16,128]{2,0,1:T(8,128)} %get-tuple-element.364) | copy-start | bytes 786436
  78.2 12.9 %all-to-all-start.2 = ((f32[16,1,4096]{2,1,0:T(1,128)}), f32[16,1,4096]{2,1,0:T(1,128)}, u32[]{:S(2)}, u32[]{:S(2)}) async-start(f32[16,1,4096]{2,1,0:T(1,128)} %reshape.3598), calls=%async_computation.2 | async-start | bytes 524288 | tf_op jit(solution)/shard_map/all_to_all | solution.py:90
  83.9 17.2 %copy-start.30 = (f32[32,16,128]{2,1,0:T(8,128)}, f32[32,16,128]{2,1,0:T(8,128)S(1)}, u32[]{:S(2)}) copy-start(f32[32,16,128]{2,1,0:T(8,128)S(1)} %copy.1633) | copy-start | bytes 786436
  85.1 17.0 %copy-start.32 = (f32[32,16,128]{2,1,0:T(8,128)}, f32[32,16,128]{2,1,0:T(8,128)S(1)}, u32[]{:S(2)}) copy-start(f32[32,16,128]{2,1,0:T(8,128)S(1)} %copy.1632) | copy-start | bytes 786436
  104.7 20.8 %copy-start = (f32[14,16,16,128]{3,2,1,0:T(8,128)S(1)}, f32[14,16,16,128]{3,2,1,0:T(8,128)}, u32[]{:S(2)}) copy-start(f32[14,16,16,128]{3,2,1,0:T(8,128)} %constant_dynamic-update-slice_fusion.13) | copy-start | bytes 5505028
  138.7 18.9 %copy-start.1 = (f32[14,16,16,128]{3,2,1,0:T(8,128)S(1)}, f32[14,16,16,128]{3,2,1,0:T(8,128)}, u32[]{:S(2)}) copy-start(f32[14,16,16,128]{3,2,1,0:T(8,128)} %constant_dynamic-update-slice_fusion.69) | copy-start | bytes 5505028
  (161 other events, 198.9 us)
where the time goes:
time: 223 us; the launch traced here: 219 us
  other arithmetic  63.6 us (29%)
  blocking collectives  63.3 us (28%)
  local copies, waits for them, and re-layouts  57.4 us (26%)
  starting transfers between devices  18.6 us (8%)
  waiting for transfers between devices  10 us (4%)
  between operations  6 us (3%)
    all_gather x2, blocking collectives, coupled(): gathered = lax.all_gather(boundary[None], 'xs', axis=0, tiled=True)  39.2 us
    unnamed x80, other arithmetic  26.3 us
    unnamed x406, local copies, waits for them, and re-layouts  21.7 us
    all_to_all x1, blocking collectives, to_lines(): return lax.all_to_all(values, 'pl', split_axis=1, concat_axis=2, tiled=True)  12.3 us
    all_to_all x1, blocking collectives, to_planes(): return lax.all_to_all(values, 'pl', split_axis=2, concat_axis=1, tiled=True)  11.8 us
    add x2, other arithmetic, matrix_vector(): matrix[2] * vector[0] + matrix[3] * vector[1]  10.1 us
    slice x42, local copies, waits for them, and re-layouts, halves(): return (paired[..., 0], paired[..., 1])  9.86 us
    all_to_all x1, starting transfers between devices, shards(): lax.all_to_all(northward_rate, 'pl', split_axis=1, concat_axis=2, tiled=T...  7.38 us
  transfers between devices with their start and end apart: 3, of which 2 were waited for; matrix products, arithmetic and copies ran while one was open for 11% of the time, Pallas kernels for 0%

commit v1 on v0

--- a/solution.py
+++ b/solution.py
@@ -212,7 +212,9 @@
 
 def coupled(boundary):
     devices = lax.axis_size("xs")
-    gathered = lax.all_gather(boundary[None], "xs", axis=0, tiled=True)
+    gathered = jnp.concatenate(
+        lax.all_to_all(jnp.stack([boundary[None]] * lax.axis_size("xs")), "xs", 0, 0), axis=0
+    )
     last_before, first_after = solve_gathered(gathered, lax.axis_index("xs"), devices)
     return (last_before, first_after)
 

time: 223 us -> 275 us (1.23)
  the two profiles are of different devices: /device:TPU:32 before, /device:TPU:1 now
where the time goes in v1:
time: 275 us; the launch traced here: 270 us
  local copies, waits for them, and re-layouts  83.8 us (30%)
  other arithmetic  71.3 us (26%)
  waiting for transfers between devices  51.1 us (19%)
  starting transfers between devices  35.5 us (13%)
  blocking collectives  22.2 us (8%)
  between operations  5.81 us (2%)
    all_to_all x2, waiting for transfers between devices, coupled(): lax.all_to_all(jnp.stack([boundary[None]] * lax.axis_size('xs')), 'xs', 0...  43 us
    unnamed x430, local copies, waits for them, and re-layouts  38.9 us
    unnamed x80, other arithmetic  31 us
    all_to_all x2, starting transfers between devices, coupled(): lax.all_to_all(jnp.stack([boundary[None]] * lax.axis_size('xs')), 'xs', 0...  16.9 us
    all_to_all x1, blocking collectives, to_planes(): return lax.all_to_all(values, 'pl', split_axis=2, concat_axis=1, tiled=True)  11.4 us
    add x2, other arithmetic, matrix_vector(): matrix[2] * vector[0] + matrix[3] * vector[1]  11.2 us
    all_to_all x1, blocking collectives, to_lines(): return lax.all_to_all(values, 'pl', split_axis=1, concat_axis=2, tiled=True)  10.8 us
    slice x42, local copies, waits for them, and re-layouts, halves(): return (paired[..., 0], paired[..., 1])  9.85 us
  transfers between devices with their start and end apart: 5, of which 4 were waited for; matrix products, arithmetic and copies ran while one was open for 9% of the time, Pallas kernels for 0%

profile of v1, /device:TPU:1, one launch (start us, length us, event | category | flops | bytes accessed | tf_op | source)
XLA Modules:
  0.0 269.7 jit_solution(8541832809988350474)
XLA Ops:
  4.0 7.6 %all-to-all-start = ((f32[32,16,128]{2,0,1:T(8,128)}), f32[32,16,128]{2,0,1:T(8,128)S(1)}, u32[]{:S(2)}, u32[]{:S(2)}) async-start(f32[32,16,128]{2,0,1:T(8,128)} %bitcast.68), calls=%async_computation | async-start | bytes 524288 | tf_op jit(solution)/shard_map/all_to_all | solution.py:86
  27.3 6.8 %all-to-all-start.1 = ((f32[32,16,128]{2,0,1:T(8,128)}), f32[32,16,128]{2,0,1:T(8,128)S(1)}, u32[]{:S(2)}, u32[]{:S(2)}) async-start(f32[32,16,128]{2,0,1:T(8,128)} %copy.1520), calls=%async_computation.1 | async-start | bytes 524288 | tf_op jit(solution)/shard_map/all_to_all | solution.py:259
  36.9 4.7 %all-to-all-done.1 = f32[32,16,128]{2,0,1:T(8,128)S(1)} async-done(((f32[32,16,128]{2,0,1:T(8,128)}), f32[32,16,128]{2,0,1:T(8,128)S(1)}, u32[]{:S(2)}, u32[]{:S(2)}) %all-to-all-start.1) | async-done | bytes 262176 | tf_op jit(solution)/shard_map/all_to_all | solution.py:259
  45.1 2.6 copy_select_fusion
  62.0 11.6 %reduce = f32[2048,32]{1,0:T(8,128)} reduce(f32[2048,1,32]{2,1,0:T(1,128)} %bitcast.4702, f32[]{:T(128)} %broadcast.2037), dimensions={1}, to_apply=%bitcast.4049.reduce_sub_computation | reduce | bytes 524292
  73.6 2.4 reshape.3608
  76.0 4.2 %all-to-all-start.2 = ((f32[16,1,4096]{2,1,0:T(1,128)}), f32[16,1,4096]{2,1,0:T(1,128)}, u32[]{:S(2)}, u32[]{:S(2)}) async-start(f32[16,1,4096]{2,1,0:T(1,128)} %reshape.3608), calls=%async_computation.2 | async-start | bytes 524288 | tf_op jit(solution)/shard_map/all_to_all | solution.py:90
  84.5 3.4 %all-to-all-done.2 = f32[16,1,4096]{2,1,0:T(1,128)} async-done(((f32[16,1,4096]{2,1,0:T(1,128)}), f32[16,1,4096]{2,1,0:T(1,128)}, u32[]{:S(2)}, u32[]{:S(2)}) %all-to-all-start.2) | async-done | bytes 262176 | tf_op jit(solution)/shard_map/all_to_all | solution.py:90
  87.9 2.9 %reduce.1 = f32[16,4096]{1,0:T(8,128)} reduce(f32[16,1,4096]{2,1,0:T(1,128)} %all-to-all-done.2, f32[]{:T(128)} %broadcast.2037), dimensions={1}, to_apply=%all_to_all.18.reduce_sub_computation | reduce | bytes 524292 | tf_op jit(solution)/shard_map/all_to_all | solution.py:90
  90.8 3.8 %reshape.3609 = f32[2048,1,32]{2,1,0:T(1,128)} reshape(f32[16,4096]{1,0:T(8,128)} %reduce.1) | data formatting | bytes 524288
  94.5 3.4 %copy.1600 = f32[32,1,2048]{2,1,0:T(1,128)} copy(f32[32,1,2048]{0,1,2:T(1,128)} %bitcast.4699) | data formatting | bytes 524288 | tf_op jit(solution)/shard_map/all_to_all | solution.py:90
  103.7 12.7 %all-to-all-start.3 = ((f32[16,1,6,16,128]{4,3,2,1,0:T(8,128)}), f32[16,1,6,16,128]{4,3,2,1,0:T(8,128)}, u32[]{:S(2)}, u32[]{:S(2)}) async-start(f32[16,1,6,16,128]{4,3,2,1,0:T(8,128)} %stack.418), calls=%async_computation.3 | async-start | bytes 1572864 | tf_op jit(solution)/shard_map/all_to_all | solution.py:216
  117.1 21.9 %all-to-all-done.3 = f32[16,1,6,16,128]{4,3,2,1,0:T(8,128)} async-done(((f32[16,1,6,16,128]{4,3,2,1,0:T(8,128)}), f32[16,1,6,16,128]{4,3,2,1,0:T(8,128)}, u32[]{:S(2)}, u32[]{:S(2)}) %all-to-all-start.3) | async-done | bytes 786464 | tf_op jit(solution)/shard_map/all_to_all | solution.py:216
  149.7 2.3 fusion.576
  163.5 6.2 %fusion.406 = (f32[16,16,128]{2,1,0:T(8,128)S(1)}, f32[16,16,128]{2,1,0:T(8,128)S(1)}, f32[16,16,128]{2,1,0:T(8,128)S(1)}, f32[16,16,128]{2,1,0:T(8,128)S(1)}, f...) fusion(f32[16,16,128]{2,1,0:T(8,128)S(1)} %get-tuple-element.322, ...), kind=kLoop, calls=%fused_computation.1275 | loop fusion | flops 23101440 | bytes 16613376 | tf_op jit(solution)/shard_map/add | solution.py:115
  175.2 4.2 %all-to-all-start.4 = ((f32[16,1,6,16,128]{4,3,2,1,0:T(8,128)}), f32[16,1,6,16,128]{4,3,2,1,0:T(8,128)}, u32[]{:S(2)}, u32[]{:S(2)}) async-start(f32[16,1,6,16,128]{4,3,2,1,0:T(8,128)} %stack.435), calls=%async_computation.4 | async-start | bytes 1572864 | tf_op jit(solution)/shard_map/all_to_all | solution.py:216
  180.0 21.1 %all-to-all-done.4 = f32[16,1,6,16,128]{4,3,2,1,0:T(8,128)} async-done(((f32[16,1,6,16,128]{4,3,2,1,0:T(8,128)}), f32[16,1,6,16,128]{4,3,2,1,0:T(8,128)}, u32[]{:S(2)}, u32[]{:S(2)}) %all-to-all-start.4) | async-done | bytes 786464 | tf_op jit(solution)/shard_map/all_to_all | solution.py:216
  208.5 2.3 fusion.572
  215.6 5.0 %fusion.403 = (f32[16,16,128]{2,1,0:T(8,128)S(1)}, f32[16,16,128]{2,1,0:T(8,128)S(1)}, f32[16,16,128]{2,1,0:T(8,128)S(1)}, f32[16,16,128]{2,1,0:T(8,128)S(1)}, f...) fusion(f32[16,16,128]{2,1,0:T(8,128)S(1)} %get-tuple-element.316, ...), kind=kLoop, calls=%fused_computation.1183 | loop fusion | flops 23101440 | bytes 16613376 | tf_op jit(solution)/shard_map/add | solution.py:115
  220.9 10.8 %all_to_all.58 = f32[32,16,128]{2,0,1:T(8,128)S(1)} all-to-all(f32[32,16,128]{2,0,1:T(8,128)S(1)} %copy.1684), channel_id=1, replica_groups=mesh['pl'=16,'xs'=16] {'pl'}, dimensions={1} | all-to-all | bytes 524288 | tf_op jit(solution)/shard_map/all_to_all | solution.py:86
  233.1 2.5 fusion.578
  241.8 9.3 %reduce.2 = f32[2048,32]{1,0:T(8,128)S(1)} reduce(f32[2048,1,32]{2,1,0:T(1,128)S(1)} %bitcast.4704, f32[]{:T(128)} %broadcast.2037), dimensions={1}, to_apply=%bitcast.4051.reduce_sub_computation | reduce | bytes 524292
  251.6 11.4 %all_to_all.59 = f32[16,1,4096]{2,1,0:T(1,128)S(1)} all-to-all(f32[16,1,4096]{2,1,0:T(1,128)S(1)} %reshape.3610), channel_id=1, replica_groups=mesh['pl'=16,'xs'=16] {'pl'}, dimensions={0} | all-to-all | bytes 524288 | tf_op jit(solution)/shard_map/all_to_all | solution.py:90
  264.3 1.8 reshape.3611
  (922 shorter events, 98.9 us)
Async XLA Ops:
  2.9 8.6 %copy-start.121 = (f32[32,16,128]{2,1,0:T(8,128)S(1)}, f32[32,16,128]{2,1,0:T(8,128)}, u32[]{:S(2)}) copy-start(f32[32,16,128]{2,1,0:T(8,128)} %param.6) | copy-start | bytes 786436
  4.0 23.3 %all-to-all-start = ((f32[32,16,128]{2,0,1:T(8,128)}), f32[32,16,128]{2,0,1:T(8,128)S(1)}, u32[]{:S(2)}, u32[]{:S(2)}) async-start(f32[32,16,128]{2,0,1:T(8,128)} %bitcast.68), calls=%async_computation | async-start | bytes 524288 | tf_op jit(solution)/shard_map/all_to_all | solution.py:86
  14.4 11.4 %copy-start.120 = (f32[32,16,128]{2,1,0:T(8,128)S(1)}, f32[32,16,128]{2,1,0:T(8,128)}, u32[]{:S(2)}) copy-start(f32[32,16,128]{2,1,0:T(8,128)} %param.7) | copy-start | bytes 786436
  17.9 9.4 %copy-start.164 = (f32[1,2,1,16,128]{4,3,2,1,0:T(8,128)}, f32[1,2,1,16,128]{4,3,2,1,0:T(8,128)S(1)}, u32[]{:S(2)}) copy-start(f32[1,2,1,16,128]{4,3,2,1,0:T(8,128)S(1)} %fusion.497) | copy-start | bytes 49156
  27.3 14.4 %all-to-all-start.1 = ((f32[32,16,128]{2,0,1:T(8,128)}), f32[32,16,128]{2,0,1:T(8,128)S(1)}, u32[]{:S(2)}, u32[]{:S(2)}) async-start(f32[32,16,128]{2,0,1:T(8,128)} %copy.1520), calls=%async_computation.1 | async-start | bytes 524288 | tf_op jit(solution)/shard_map/all_to_all | solution.py:259
  50.7 8.1 %copy-start = (f32[32,1,512,1]{0,3,2,1:T(1,128)}, f32[32,1,512,1]{0,3,2,1:T(1,128)S(1)}, u32[]{:S(2)}) copy-start(f32[32,1,512,1]{0,3,2,1:T(1,128)S(1)} %get-tuple-element.347) | copy-start | bytes 196612
  51.2 7.6 %copy-start.2 = (f32[32,1,512,1]{0,3,2,1:T(1,128)}, f32[32,1,512,1]{0,3,2,1:T(1,128)S(1)}, u32[]{:S(2)}) copy-start(f32[32,1,512,1]{0,3,2,1:T(1,128)S(1)} %get-tuple-element.343) | copy-start | bytes 196612
  52.5 5.9 %copy-start.18 = (f32[32,1,256,1]{0,3,2,1:T(1,128)}, f32[32,1,256,1]{0,3,2,1:T(1,128)S(1)}, u32[]{:S(2)}) copy-start(f32[32,1,256,1]{0,3,2,1:T(1,128)S(1)} %get-tuple-element.372) | copy-start | bytes 98308
  52.8 5.7 %copy-start.20 = (f32[32,1,256,1]{0,3,2,1:T(1,128)}, f32[32,1,256,1]{0,3,2,1:T(1,128)S(1)}, u32[]{:S(2)}) copy-start(f32[32,1,256,1]{0,3,2,1:T(1,128)S(1)} %get-tuple-element.368) | copy-start | bytes 98308
  53.2 5.0 %copy-start.12 = (f32[32,1,128,1]{0,3,2,1:T(1,128)}, f32[32,1,128,1]{0,3,2,1:T(1,128)S(1)}, u32[]{:S(2)}) copy-start(f32[32,1,128,1]{0,3,2,1:T(1,128)S(1)} %get-tuple-element.399) | copy-start | bytes 49156
  53.6 4.6 %copy-start.39 = (f32[32,1,128,1]{0,3,2,1:T(1,128)}, f32[32,1,128,1]{0,3,2,1:T(1,128)S(1)}, u32[]{:S(2)}) copy-start(f32[32,1,128,1]{0,3,2,1:T(1,128)S(1)} %get-tuple-element.400) | copy-start | bytes 49156
  53.8 4.5 %copy-start.41 = (f32[32,1,128,1]{0,3,2,1:T(1,128)}, f32[32,1,128,1]{0,3,2,1:T(1,128)S(1)}, u32[]{:S(2)}) copy-start(f32[32,1,128,1]{0,3,2,1:T(1,128)S(1)} %get-tuple-element.396) | copy-start | bytes 49156
  54.0 4.0 %copy-start.33 = (f32[32,1,64,1]{0,3,2,1:T(1,128)}, f32[32,1,64,1]{0,3,2,1:T(1,128)S(1)}, u32[]{:S(2)}) copy-start(f32[32,1,64,1]{0,3,2,1:T(1,128)S(1)} %get-tuple-element.417) | copy-start | bytes 24580
  54.6 3.7 %copy-start.72 = (f32[32,1,64,1]{0,3,2,1:T(1,128)}, f32[32,1,64,1]{0,3,2,1:T(1,128)S(1)}, u32[]{:S(2)}) copy-start(f32[32,1,64,1]{0,3,2,1:T(1,128)S(1)} %get-tuple-element.414) | copy-start | bytes 24580
  54.6 3.7 %copy-start.108 = (f32[32,1,64]{0,2,1:T(8,128)}, f32[32,1,64]{0,2,1:T(8,128)S(1)}, u32[]{:S(2)}) copy-start(f32[32,1,64]{0,2,1:T(8,128)S(1)} %get-tuple-element.236) | copy-start | bytes 24580
  62.0 18.2 %copy-start.165 = (f32[1,2,1,16,128]{4,3,2,1,0:T(8,128)S(1)}, f32[1,2,1,16,128]{4,3,2,1,0:T(8,128)}, u32[]{:S(2)}) copy-start(f32[1,2,1,16,128]{4,3,2,1,0:T(8,128)} %copy-done.164) | copy-start | bytes 49156
  62.0 18.8 %copy-start.60 = (f32[16,1,1,16,128]{4,1,0,3,2:T(1,128)S(1)}, f32[16,1,1,16,128]{4,1,0,3,2:T(1,128)}, u32[]{:S(2)}) copy-start(f32[16,1,1,16,128]{4,1,0,3,2:T(1,128)} %copy-done.59) | copy-start | bytes 393220
  62.0 19.5 %copy-start.67 = (f32[32,16,128]{2,0,1:T(8,128)S(1)}, f32[32,16,128]{2,0,1:T(8,128)}, u32[]{:S(2)}) copy-start(f32[32,16,128]{2,0,1:T(8,128)} %get-tuple-element.364) | copy-start | bytes 786436
  76.0 11.8 %all-to-all-start.2 = ((f32[16,1,4096]{2,1,0:T(1,128)}), f32[16,1,4096]{2,1,0:T(1,128)}, u32[]{:S(2)}, u32[]{:S(2)}) async-start(f32[16,1,4096]{2,1,0:T(1,128)} %reshape.3608), calls=%async_computation.2 | async-start | bytes 524288 | tf_op jit(solution)/shard_map/all_to_all | solution.py:90
  103.7 35.4 %all-to-all-start.3 = ((f32[16,1,6,16,128]{4,3,2,1,0:T(8,128)}), f32[16,1,6,16,128]{4,3,2,1,0:T(8,128)}, u32[]{:S(2)}, u32[]{:S(2)}) async-start(f32[16,1,6,16,128]{4,3,2,1,0:T(8,128)} %stack.418), calls=%async_computation.3 | async-start | bytes 1572864 | tf_op jit(solution)/shard_map/all_to_all | solution.py:216
  163.5 6.3 %copy-start.15 = (f32[16,2,3,16,128]{4,3,2,1,0:T(8,128)S(1)}, f32[16,2,3,16,128]{4,3,2,1,0:T(8,128)}, u32[]{:S(2)}) copy-start(f32[16,2,3,16,128]{4,3,2,1,0:T(8,128)} %copy-done.14) | copy-start | bytes 2359300
  175.2 25.9 %all-to-all-start.4 = ((f32[16,1,6,16,128]{4,3,2,1,0:T(8,128)}), f32[16,1,6,16,128]{4,3,2,1,0:T(8,128)}, u32[]{:S(2)}, u32[]{:S(2)}) async-start(f32[16,1,6,16,128]{4,3,2,1,0:T(8,128)} %stack.435), calls=%async_computation.4 | async-start | bytes 1572864 | tf_op jit(solution)/shard_map/all_to_all | solution.py:216
  215.6 5.1 %copy-start.159 = (f32[1,16,128]{2,1,0:T(8,128)S(1)}, f32[1,16,128]{2,1,0:T(8,128)}, u32[]{:S(2)}) copy-start(f32[1,16,128]{2,1,0:T(8,128)} %copy-done.158) | copy-start | bytes 24580
  215.6 5.2 %copy-start.17 = (f32[16,2,3,16,128]{4,3,2,1,0:T(8,128)S(1)}, f32[16,2,3,16,128]{4,3,2,1,0:T(8,128)}, u32[]{:S(2)}) copy-start(f32[16,2,3,16,128]{4,3,2,1,0:T(8,128)} %copy-done.16) | copy-start | bytes 2359300
  (175 other events, 226.2 us)
